TPU v7x, 32 devices: a whole 2x2x4 slice. The times are simulated.
32 devices in a mesh: groups: 2 (over x), expert: 8 (over z, y), helper: 2 (over core).
Axes of the slice: x: 2, y: 2, z: 4, core: 2. Of those that a mesh axis runs over, the one named last changes fastest.
Arguments:
- slot_rows: bfloat16 [12288, 4096], P(('groups', 'expert', 'helper')), parts along dimension 0, may hold values from -6 to 6
- experts: int32 [3072, 2], P(('groups', 'expert', 'helper')), parts along dimension 0, may hold values from 0 to 7, all different within a row; in each aligned block of 96 rows (0 to 95, 96 to 191, ...) at most 48 rows name the same one
- gate_values: float32 [3072, 2], P(('groups', 'expert', 'helper')), parts along dimension 0, may hold values from 0.1 to 1
- gate_weight: bfloat16 [8, 4096, 768], P('expert', None, 'helper'), may hold values from -0.09375 to 0.09375
- up_weight: bfloat16 [8, 4096, 768], P('expert', None, 'helper'), may hold values from -0.09375 to 0.09375
- down_weight: bfloat16 [8, 768, 4096], P('expert', 'helper'), may hold values from -0.21875 to 0.21875
Outputs:
- layer_output: bfloat16 [3072, 4096], P(('groups', 'expert', 'helper')), parts along dimension 0
There are 2 independent parts, one for each index of `groups`. A program takes and returns all parts, laid end to end along the dimension named above; an argument that names none is the same for every part. Nothing has to cross between parts.
Inputs may be any that keep to these rules, and one draw needn't show every extreme that they name: Each row names 2 different experts. Within the rows of one token block no expert is named by more than 48 rows, and in some block one expert is named by exactly 48 rows. Every expert is named by some row.
All inputs are finite; a program needn't handle non-finite values.
Results may differ from a plain program's by a relative error of at most 0.0058.
Values may be sent and summed in bfloat16 or wider, within the bound.
A program may use at most 128 MiB of HBM per device.

v0:
```python
import jax
import jax.numpy as jnp
from jax import lax
from jax.sharding import PartitionSpec as P


def shards(slot_rows, experts, gate_values, gate_weight, up_weight, down_weight):
    gate_part = gate_weight[0]
    up_part = up_weight[0]
    down_part = down_weight[0]
    expert_count = lax.axis_size("expert")
    per_source = slot_rows.shape[0] // expert_count
    onehot = (
        experts[:, :, None] == jnp.arange(expert_count, dtype=jnp.int32)[None, None, :]
    ).astype(jnp.int32)
    per_token = jnp.sum(onehot, axis=1)
    before = jnp.cumsum(per_token, axis=0) - per_token
    within = jnp.take_along_axis(before, experts, axis=1)
    local_slot = experts * per_source + within
    inputs = lax.all_gather(slot_rows, "helper", axis=0, tiled=True)
    gated = jnp.dot(inputs, gate_part, preferred_element_type=jnp.float32)
    lifted = jnp.dot(inputs, up_part, preferred_element_type=jnp.float32)
    hidden = (jax.nn.silu(gated) * lifted).astype(jnp.bfloat16)
    own_rows = lax.all_to_all(hidden, "helper", split_axis=0, concat_axis=1, tiled=True)
    outputs = jnp.dot(
        own_rows,
        lax.all_gather(down_part, "helper", axis=0, tiled=True),
        preferred_element_type=jnp.float32,
    ).astype(jnp.bfloat16)
    received = lax.all_to_all(outputs, "expert", split_axis=0, concat_axis=0, tiled=True)
    picked = received[local_slot]
    combined = jnp.sum(gate_values[:, :, None] * picked.astype(jnp.float32), axis=1)
    return combined.astype(jnp.bfloat16)


def solution(mesh):
    return jax.shard_map(
        shards,
        mesh=mesh,
        in_specs=(
            P(("groups", "expert", "helper"), None),
            P(("groups", "expert", "helper"), None),
            P(("groups", "expert", "helper"), None),
            P("expert", None, "helper"),
            P("expert", None, "helper"),
            P("expert", "helper", None),
        ),
        out_specs=P(("groups", "expert", "helper"), None),
        check_vma=False,
    )
```

profile of v0, /device:TPU:0, one launch (start us, length us, event | category | flops | bytes accessed | tf_op | source)
XLA Modules:
  0.0 158.5 jit_solution(8802053274376082575)
XLA Ops:
  6.5 0.0 copy-start
  6.5 0.0 all-gather.4.cloned.1.call-start
  6.5 0.7 all-gather.4.cloned.1.call-update
  7.3 0.0 all-gather.6.cloned.1.call-start
  7.3 0.7 all-gather.6.cloned.1.call-update
  8.0 20.4 %all-gather.4.cloned.1.call-done = bf16[768,4096]{1,0:T(8,128)(2,1)} async-done(((bf16[384,4096]{1,0:T(8,128)(2,1)}), bf16[768,4096]{1,0:T(8,128)(2,1)}) %all-gather.4.cloned.1.call-update) | async-done | bytes 6291472 | tf_op jit(solution)/shard_map/all_gather | solution.py:20
  28.4 0.0 copy-done
  28.4 0.0 copy-start.3
  28.4 0.0 copy-start.4
  28.4 6.0 %fusion.7 = f32[768,384]{1,0:T(8,128)S(1)} fusion(bf16[768,4096]{1,0:T(8,128)(2,1)} %all-gather.4.cloned.1.call-done, bf16[1,4096,384]{2,1,0:T(8,128)(2,1)S(1)} %copy-done), kind=kOutput, calls=%fused_computation.7 | convolution fusion | flops 2415919104 | bytes 10616832 | tf_op jit(solution)/shard_map/dot_general | solution.py:21
  34.5 0.0 copy-done.3
  34.5 0.0 copy-done.4
  34.5 4.3 %fusion.12 = bf16[768,384]{1,0:T(8,128)(2,1)} fusion(bf16[768,4096]{1,0:T(8,128)(2,1)S(1)} %copy-done.3, bf16[1,4096,384]{2,1,0:T(8,128)(2,1)S(1)} %copy-done.4, f32[768,384]{1,0:T(8,128)S(1)} %fusion.7), kind=kOutput, calls=%fused_computation.11 | convolution fusion | flops 2417688576 | bytes 11206656 | tf_op jit(solution)/shard_map/dot_general | solution.py:22
  38.8 2.2 %copy.31 = bf16[2,384,384]{1,2,0:T(8,128)(2,1)} copy(bf16[2,384,384]{2,1,0:T(8,128)(2,1)} %bitcast.30) | data formatting | bytes 1179648 | tf_op jit(solution)/shard_map/all_to_all | solution.py:24
  41.0 6.6 %all_to_all.31 = bf16[2,384,384]{1,2,0:T(8,128)(2,1)} all-to-all(bf16[2,384,384]{1,2,0:T(8,128)(2,1)} %copy.31), channel_id=1, replica_groups=mesh['groups'=2,'expert'=8,'helper'=2] {'helper'}, dimensions={0} | all-to-all | bytes 1179648 | tf_op jit(solution)/shard_map/all_to_all | solution.py:24
  47.6 0.7 all-gather.6.cloned.1.call-done
  48.3 7.3 %fusion.2 = bf16[384,4096]{1,0:T(8,128)(2,1)} fusion(bf16[384,768]{0,1:T(8,128)(2,1)} %bitcast.29, bf16[1,768,4096]{2,1,0:T(8,128)(2,1)} %all-gather.6.cloned.1.call-done), kind=kOutput, calls=%fused_computation.4 | convolution fusion | flops 2417491968 | bytes 10027008 | tf_op jit(solution)/shard_map/dot_general | solution.py:25
  55.6 0.0 copy-start.1
  55.6 5.9 %all-to-all-start.1 = ((bf16[8,48,4096]{2,1,0:T(8,128)(2,1)}), bf16[8,48,4096]{2,1,0:T(8,128)(2,1)}, u32[]{:S(2)}, u32[]{:S(2)}) async-start(bf16[8,48,4096]{2,1,0:T(8,128)(2,1)} %bitcast.28), calls=%async_computation.1 | async-start | bytes 6291456 | tf_op jit(solution)/shard_map/all_to_all | solution.py:30
  61.6 0.0 copy-done.1
  61.6 0.1 copy.32
  61.7 0.1 reduce_window_sum.11
  61.8 0.1 copy.34
  61.9 0.1 reshape.25
  62.1 0.0 copy-start.2
  62.1 1.6 %gather_fusion.1 = s32[192]{0:T(256)S(1)} fusion(s32[96,8]{1,0:T(8,128)S(1)} %sub.3, s32[192]{0:T(256)S(1)} %reshape.25), kind=kCustom, calls=%fused_computation.1 | custom fusion | bytes 3072 | tf_op jit(solution)/shard_map/jit(take_along_axis)/gather | solution.py:18
  63.7 0.1 reshape.28
  63.8 0.1 copy.35
  63.9 0.1 copy.36
  64.0 0.1 reshape.19
  64.2 0.0 copy-done.2
  64.2 0.1 copy.30
  64.3 68.5 %all-to-all-done.1 = bf16[8,48,4096]{2,1,0:T(8,128)(2,1)} async-done(((bf16[8,48,4096]{2,1,0:T(8,128)(2,1)}), bf16[8,48,4096]{2,1,0:T(8,128)(2,1)}, u32[]{:S(2)}, u32[]{:S(2)}) %all-to-all-start.1) | async-done | bytes 3145760 | tf_op jit(solution)/shard_map/all_to_all | solution.py:30
  132.8 6.5 %gather_fusion = bf16[192,4096]{1,0:T(8,128)(2,1)} fusion(bf16[384,4096]{1,0:T(8,128)(2,1)} %bitcast.7, s32[1024]{0:T(1024)S(1)} %pad_clamp_fusion), kind=kCustom, calls=%fused_computation | custom fusion | bytes 3146496 | tf_op jit(solution)/shard_map/gather | solution.py:31
  139.3 4.7 %reshape.34 = f32[96,2,4096]{2,1,0:T(2,128)} reshape(bf16[192,4096]{1,0:T(8,128)(2,1)} %gather_fusion) | data formatting | bytes 4718592 | tf_op jit(solution)/shard_map/convert_element_type | solution.py:32
  144.1 7.6 %multiply_reduce_fusion = bf16[96,4096]{1,0:T(8,128)(2,1)} fusion(f32[96,2,4096]{2,1,0:T(2,128)} %reshape.34, f32[96,2]{1,0:T(8,128)S(1)} %copy.30), kind=kLoop, calls=%fused_computation.9 | loop fusion | flops 1179648 | bytes 3932928 | tf_op jit(solution)/shard_map/reduce_sum | solution.py:32
  (5 shorter events, 0.0 us)
Async XLA Ops:
  6.5 21.9 %copy-start = (bf16[1,4096,384]{2,1,0:T(8,128)(2,1)S(1)}, bf16[1,4096,384]{2,1,0:T(8,128)(2,1)}, u32[]{:S(2)}) copy-start(bf16[1,4096,384]{2,1,0:T(8,128)(2,1)} %param.9) | copy-start | bytes 9437188
  6.5 21.8 %all-gather.4.cloned.1.call-start = ((), (), s32[]{:S(2)}) async-start(), calls=%async_computation.2 | async-start | bytes 9437184 | tf_op jit(solution)/shard_map/all_gather | solution.py:20
  7.3 41.1 %all-gather.6.cloned.1.call-start = ((), (), s32[]{:S(2)}) async-start(), calls=%async_computation.3 | async-start | bytes 9437184 | tf_op jit(solution)/shard_map/all_gather | solution.py:27
  28.4 6.1 %copy-start.3 = (bf16[768,4096]{1,0:T(8,128)(2,1)S(1)}, bf16[768,4096]{1,0:T(8,128)(2,1)}, u32[]{:S(2)}) copy-start(bf16[768,4096]{1,0:T(8,128)(2,1)} %all-gather.4.cloned.1.call-done) | copy-start | bytes 18874372
  28.4 6.1 %copy-start.4 = (bf16[1,4096,384]{2,1,0:T(8,128)(2,1)S(1)}, bf16[1,4096,384]{2,1,0:T(8,128)(2,1)}, u32[]{:S(2)}) copy-start(bf16[1,4096,384]{2,1,0:T(8,128)(2,1)} %param.10) | copy-start | bytes 9437188
  55.6 5.9 %copy-start.1 = (s32[96,2]{0,1:T(2,128)S(1)}, s32[96,2]{0,1:T(2,128)}, u32[]{:S(2)}) copy-start(s32[96,2]{0,1:T(2,128)} %param.7) | copy-start | bytes 2308
  55.6 77.2 %all-to-all-start.1 = ((bf16[8,48,4096]{2,1,0:T(8,128)(2,1)}), bf16[8,48,4096]{2,1,0:T(8,128)(2,1)}, u32[]{:S(2)}, u32[]{:S(2)}) async-start(bf16[8,48,4096]{2,1,0:T(8,128)(2,1)} %bitcast.28), calls=%async_computation.1 | async-start | bytes 6291456 | tf_op jit(solution)/shard_map/all_to_all | solution.py:30
  62.1 2.1 %copy-start.2 = (f32[96,2]{0,1:T(2,128)S(1)}, f32[96,2]{0,1:T(2,128)}, u32[]{:S(2)}) copy-start(f32[96,2]{0,1:T(2,128)} %param.8) | copy-start | bytes 2308
Sparse Core Ops, SparseCore 0:
  8.9 19.4 all-gather.3
  29.9 18.3 all-gather.5
where the time goes:
time: 159 us; the launch traced here: 158 us
  waiting for transfers between devices  91 us (57%)
  matrix products  17.7 us (11%)
  local copies, waits for them, and re-layouts  16 us (10%)
  between operations  13.5 us (8%)
  other arithmetic  7.76 us (5%)
  blocking collectives  6.64 us (4%)
  starting transfers between devices  5.96 us (4%)
    all_to_all x1, waiting for transfers between devices, shards(): lax.all_to_all(outputs, 'expert', split_axis=0, concat_axis=0, tiled=True)  68.5 us
    all_gather x1, waiting for transfers between devices, shards(): inputs = lax.all_gather(slot_rows, 'helper', axis=0, tiled=True)  20.4 us
    reduce_sum x1, other arithmetic, shards(): jnp.sum(gate_values[:, :, None] * picked.astype(jnp.float32), axis=1)  7.59 us
    dot_general x1, matrix products, shards(): jnp.dot(own_rows, lax.all_gather(down_part, 'helper', axis=0, tiled=True)...  7.33 us
    all_to_all x1, blocking collectives, shards(): lax.all_to_all(hidden, 'helper', split_axis=0, concat_axis=1, tiled=True)  6.64 us
    gather x1, local copies, waits for them, and re-layouts, shards(): picked = received[local_slot]  6.49 us
    dot_general x1, matrix products, shards(): gated = jnp.dot(inputs, gate_part, preferred_element_type=jnp.float32)  6.05 us
    all_to_all x1, starting transfers between devices, shards(): lax.all_to_all(outputs, 'expert', split_axis=0, concat_axis=0, tiled=True)  5.92 us
  transfers between devices with their start and end apart: 3, of which 3 were waited for; matrix products, arithmetic and copies ran while one was open for 10% of the time, Pallas kernels for 0%

commit v1 on v0

--- a/solution.py
+++ b/solution.py
@@ -1,15 +1,351 @@
+import functools
 import jax
 import jax.numpy as jnp
 from jax import lax
+from jax.experimental import pallas as pl
+from jax.experimental.pallas import tpu as pltpu
 from jax.sharding import PartitionSpec as P
 
+COLUMNS = 2
+MESH = pl.DeviceIdType.MESH
+
+
+def remote(src, dst, send, recv, **where):
+    return pltpu.make_async_remote_copy(
+        src_ref=src, dst_ref=dst, send_sem=send, recv_sem=recv,
+        device_id=where, device_id_type=MESH,
+    )
+
+
+def arrival(dst, sem):
+    return pltpu.make_async_copy(dst, dst, sem)
+
+
+def weights_of(experts, gates, expert_count, width, first, slots):
+    rows, top = experts.shape
+    names = lax.broadcasted_iota(jnp.int32, (rows, expert_count), 1)
+    chosen = [(experts[:, k:k + 1] == names).astype(jnp.float32) for k in range(top)]
+    earlier = (
+        lax.broadcasted_iota(jnp.int32, (rows, rows), 0)
+        > lax.broadcasted_iota(jnp.int32, (rows, rows), 1)
+    )
+    before = jnp.dot(
+        earlier.astype(jnp.float32).astype(jnp.bfloat16),
+        sum(chosen).astype(jnp.bfloat16),
+        preferred_element_type=jnp.float32,
+    )
+    number = lax.broadcasted_iota(jnp.int32, (rows, slots), 1) + first
+    total = jnp.zeros((rows, slots), jnp.float32)
+    for k in range(top):
+        within = jnp.sum(chosen[k] * before, axis=1, keepdims=True).astype(jnp.int32)
+        slot = experts[:, k:k + 1] * width + within
+        total = total + jnp.where(number == slot, gates[:, k:k + 1], 0.0)
+    high = total.astype(jnp.bfloat16)
+    return high, (total - high.astype(jnp.float32)).astype(jnp.bfloat16)
+
+
+def layer_kernel(
+    count, depth_chunks, row_chunks, chunks,
+    x, gw, uw, dw, ex, gv, out,
+    own, other, gb, ub, db, dp, acc_g, acc_u, give, mine, theirs,
+    outb, relayed, partial, near, far, far_ex, far_gv, w_near, w_far,
+    load_sem, x_send, x_recv, h_send, h_recv, d_sem,
+    m_send, m_recv, f_send, f_recv, n_send, n_recv, p_send, p_recv,
+):
+    e, h = lax.axis_index("expert"), lax.axis_index("helper")
+    rows, width = x.shape
+    slots = rows // count
+    half = count // 2
+    lines = half // COLUMNS
+    z, y = e // COLUMNS, e % COLUMNS
+    side = e // half
+    place = e % half
+    line = place // COLUMNS
+    inner = lines - 1 + side
+    is_relay = z == inner
+    far_first = (1 - side) * lines
+    near_slots = half * slots
+    tokens = ex.shape[0]
+    depth = width // depth_chunks
+    part_rows = rows // row_chunks
+    cols_of = width // chunks
+
+    def load(k):
+        ks = pl.ds(k * depth if isinstance(k, int) else pl.multiple_of(k * depth, depth), depth)
+        return (
+            pltpu.make_async_copy(x.at[:, ks], own.at[:, ks], load_sem.at[0, k]),
+            pltpu.make_async_copy(gw.at[ks], gb.at[ks], load_sem.at[1, k]),
+            pltpu.make_async_copy(uw.at[ks], ub.at[ks], load_sem.at[2, k]),
+        )
+
+    for k in range(depth_chunks):
+        for copy in load(k):
+            copy.start()
+    down_load = pltpu.make_async_copy(dw, db, d_sem.at[0])
+    down_load.start()
+
+    barrier = pltpu.get_barrier_semaphore()
+    for step in range(1, count):
+        pl.semaphore_signal(
+            barrier, inc=1, device_id={"expert": (e + step) % count}, device_id_type=MESH
+        )
+    pl.semaphore_signal(barrier, inc=1, device_id={"helper": 1 - h}, device_id_type=MESH)
+    pl.semaphore_wait(barrier, count)
+
+    def rows_copy(r):
+        rs = pl.ds(r * part_rows, part_rows)
+        return remote(x.at[rs], other.at[rs], x_send.at[r], x_recv.at[r], helper=1 - h)
+
+    for r in range(row_chunks):
+        rows_copy(r).start()
+    down_copy = remote(dw, dp, d_sem.at[1], d_sem.at[2], helper=1 - h)
+    down_copy.start()
+
+    far_relay = (lines - side) * COLUMNS + y
+    notes = (
+        remote(ex, far_ex.at[line], m_send.at[0], m_recv.at[line, 0], expert=far_relay),
+        remote(gv, far_gv.at[line], m_send.at[1], m_recv.at[line, 1], expert=far_relay),
+    )
+    for copy in notes:
+        copy.start()
+
+    def activate(source, first, size, target, waits):
+        acc_g[pl.ds(0, size)] = jnp.zeros((size, acc_g.shape[1]), jnp.float32)
+        acc_u[pl.ds(0, size)] = jnp.zeros((size, acc_u.shape[1]), jnp.float32)
+
+        def step(k, carry):
+            ks = pl.ds(pl.multiple_of(k * depth, depth), depth)
+            if waits:
+                for copy in load(k):
+                    copy.wait()
+            block = source[pl.ds(first, size), ks]
+            acc_g[pl.ds(0, size)] += jnp.dot(block, gb[ks], preferred_element_type=jnp.float32)
+            acc_u[pl.ds(0, size)] += jnp.dot(block, ub[ks], preferred_element_type=jnp.float32)
+            return carry
+
+        lax.fori_loop(0, depth_chunks, step, 0)
+        gated = acc_g[pl.ds(0, size)]
+        hidden = gated / (1.0 + jnp.exp(-gated)) * acc_u[pl.ds(0, size)]
+        target[pl.ds(first, size)] = hidden.astype(jnp.bfloat16)
+
+    activate(own, 0, rows, mine, True)
+
+    def hidden_copy(r):
+        rs = pl.ds(r * part_rows, part_rows)
+        return remote(give.at[rs], theirs.at[rs], h_send.at[r], h_recv.at[r], helper=1 - h)
+
+    for r in range(row_chunks):
+        rows_copy(r).wait_recv()
+        activate(other, r * part_rows, part_rows, give, False)
+        hidden_copy(r).start()
+
+    w_near[0], w_near[1] = weights_of(ex[...], gv[...], count, slots, side * near_slots, near_slots)
+
+    down_load.wait()
+    down_copy.wait_recv()
+    for r in range(row_chunks):
+        hidden_copy(r).wait_recv()
+
+    def columns(c):
+        return pl.ds(pl.multiple_of(c * cols_of, cols_of), cols_of)
+
+    def rows_at(index):
+        return pl.ds(pl.multiple_of(index * slots, slots), slots)
+
+    def to_relay(c, l, step):
+        column = (y + step) % COLUMNS
+        block = (far_first + l) * COLUMNS + column
+        source = outb.at[rows_at(block), columns(c)]
+        target = relayed.at[l, rows_at(place), columns(c)]
+        sem = f_recv.at[c, l, place]
+        local = pltpu.make_async_copy(source, target, sem)
+        away = remote(
+            source, target, f_send.at[c, l, step], sem, expert=inner * COLUMNS + column
+        )
+        return local, away
+
+    def to_near(c, step):
+        goal = side * half + (place + step) % half
+        source = outb.at[rows_at(goal), columns(c)]
+        target = near.at[rows_at(place), columns(c)]
+        if step == 0:
+            return pltpu.make_async_copy(source, target, n_recv.at[c, place])
+        return remote(source, target, n_send.at[c, step], n_recv.at[c, place], expert=goal)
+
+    def to_far(c, l):
+        goal = (far_first + l) * COLUMNS + y
+        return remote(
+            partial.at[l, :, columns(c)], far.at[:, columns(c)],
+            p_send.at[c, l], p_recv.at[c], expert=goal,
+        )
+
+    def lower(c, carry):
+        cs = columns(c)
+        value = jnp.dot(mine[...], db[:, cs], preferred_element_type=jnp.float32)
+        value += jnp.dot(theirs[...], dp[:, cs], preferred_element_type=jnp.float32)
+        outb[:, cs] = value.astype(jnp.bfloat16)
+        for l in range(lines):
+            for step in range(COLUMNS):
+                local, away = to_relay(c, l, step)
+                if step:
+                    away.start()
+                else:
+                    @pl.when(is_relay)
+                    def _():
+                        local.start()
+
+                    @pl.when(jnp.logical_not(is_relay))
+                    def _():
+                        away.start()
+        return carry
+
+    lax.fori_loop(0, chunks, lower, 0)
+
+    def send_near(c, carry):
+        for step in range(half):
+            to_near(c, step).start()
+        return carry
+
+    lax.fori_loop(0, chunks, send_near, 0)
+
+    @pl.when(is_relay)
+    def _():
+        for l in range(lines):
+            arrival(far_ex.at[l], m_recv.at[l, 0]).wait()
+            arrival(far_gv.at[l], m_recv.at[l, 1]).wait()
+            w_far[l, 0], w_far[l, 1] = weights_of(
+                far_ex[l], far_gv[l], count, slots, side * near_slots, near_slots
+            )
+
+        def relay(c, carry):
+            cs = columns(c)
+            for l in range(lines):
+                for s in range(half):
+                    arrival(relayed.at[l, pl.ds(s * slots, slots), cs], f_recv.at[c, l, s]).wait()
+                block = relayed[l, :, cs]
+                value = jnp.dot(w_far[l, 0], block, preferred_element_type=jnp.float32)
+                value += jnp.dot(w_far[l, 1], block, preferred_element_type=jnp.float32)
+                partial[l, :, cs] = value.astype(jnp.bfloat16)
+                to_far(c, l).start()
+            return carry
+
+        lax.fori_loop(0, chunks, relay, 0)
+
+    def combine(c, carry):
+        cs = columns(c)
+        for s in range(half):
+            arrival(near.at[pl.ds(s * slots, slots), cs], n_recv.at[c, s]).wait()
+        block = near[:, cs]
+        value = jnp.dot(w_near[0], block, preferred_element_type=jnp.float32)
+        value += jnp.dot(w_near[1], block, preferred_element_type=jnp.float32)
+        arrival(far.at[:, cs], p_recv.at[c]).wait()
+        out[:, cs] = (value + far[:, cs].astype(jnp.float32)).astype(jnp.bfloat16)
+        return carry
+
+    lax.fori_loop(0, chunks, combine, 0)
+
+    def finish(c, carry):
+        for l in range(lines):
+            for step in range(COLUMNS):
+                away = to_relay(c, l, step)[1]
+                if step:
+                    away.wait_send()
+                else:
+                    @pl.when(jnp.logical_not(is_relay))
+                    def _():
+                        away.wait_send()
+        for step in range(1, half):
+            to_near(c, step).wait_send()
+
+        @pl.when(is_relay)
+        def _():
+            for l in range(lines):
+                to_far(c, l).wait_send()
+        return carry
+
+    lax.fori_loop(0, chunks, finish, 0)
+    for r in range(row_chunks):
+        rows_copy(r).wait_send()
+        hidden_copy(r).wait_send()
+    down_copy.wait_send()
+    for copy in notes:
+        copy.wait_send()
+
+
+def fused(slot_rows, experts, gate_values, gate_weight, up_weight, down_weight):
+    count = lax.axis_size("expert")
+    rows, width = slot_rows.shape
+    units = gate_weight.shape[2]
+    tokens, top = experts.shape
+    slots = rows // count
+    half = count // 2
+    lines = half // COLUMNS
+    near_slots = half * slots
+    depth_chunks, row_chunks, chunks = 4, 2, 8
+    bf16, f32 = jnp.bfloat16, jnp.float32
+    dma = pltpu.SemaphoreType.DMA
+    vmem = pl.BlockSpec(memory_space=pltpu.VMEM)
+    hbm = pl.BlockSpec(memory_space=pl.ANY)
+    return pl.pallas_call(
+        functools.partial(layer_kernel, count, depth_chunks, row_chunks, chunks),
+        out_shape=jax.ShapeDtypeStruct((tokens, width), bf16),
+        in_specs=[hbm, hbm, hbm, hbm, vmem, vmem],
+        out_specs=vmem,
+        scratch_shapes=[
+            pltpu.VMEM((rows, width), bf16),
+            pltpu.VMEM((rows, width), bf16),
+            pltpu.VMEM((width, units), bf16),
+            pltpu.VMEM((width, units), bf16),
+            pltpu.VMEM((units, width), bf16),
+            pltpu.VMEM((units, width), bf16),
+            pltpu.VMEM((rows, units), f32),
+            pltpu.VMEM((rows, units), f32),
+            pltpu.VMEM((rows, units), bf16),
+            pltpu.VMEM((rows, units), bf16),
+            pltpu.VMEM((rows, units), bf16),
+            pltpu.VMEM((rows, width), bf16),
+            pltpu.VMEM((lines, near_slots, width), bf16),
+            pltpu.VMEM((lines, tokens, width), bf16),
+            pltpu.VMEM((near_slots, width), bf16),
+            pltpu.VMEM((tokens, width), bf16),
+            pltpu.VMEM((lines, tokens, top), jnp.int32),
+            pltpu.VMEM((lines, tokens, top), f32),
+            pltpu.VMEM((2, tokens, near_slots), bf16),
+            pltpu.VMEM((lines, 2, tokens, near_slots), bf16),
+            dma((3, depth_chunks)),
+            dma((row_chunks,)), dma((row_chunks,)),
+            dma((row_chunks,)), dma((row_chunks,)),
+            dma((3,)),
+            dma((2,)), dma((lines, 2)),
+            dma((chunks, lines, COLUMNS)), dma((chunks, lines, half)),
+            dma((chunks, half)), dma((chunks, half)),
+            dma((chunks, lines)), dma((chunks,)),
+        ],
+        compiler_params=pltpu.CompilerParams(
+            collective_id=0, has_side_effects=True, vmem_limit_bytes=60 << 20
+        ),
+        name="expert_layer",
+    )(
+        slot_rows,
+        gate_weight.reshape(gate_weight.shape[1:]),
+        up_weight.reshape(up_weight.shape[1:]),
+        down_weight.reshape(down_weight.shape[1:]),
+        experts,
+        gate_values,
+    )
+
 
 def shards(slot_rows, experts, gate_values, gate_weight, up_weight, down_weight):
+    tile = 16
+    expert_count = lax.axis_size("expert")
+    per_source = slot_rows.shape[0] // expert_count
+    if per_source % tile == 0 and expert_count % (2 * COLUMNS) == 0:
+        return fused(
+            slot_rows, experts, gate_values, gate_weight, up_weight, down_weight
+        )
     gate_part = gate_weight[0]
     up_part = up_weight[0]
     down_part = down_weight[0]
-    expert_count = lax.axis_size("expert")
-    per_source = slot_rows.shape[0] // expert_count
     onehot = (
         experts[:, :, None] == jnp.arange(expert_count, dtype=jnp.int32)[None, None, :]
     ).astype(jnp.int32)

time: 159 us -> 76.5 us (0.48)
  waiting for transfers between devices: 91 us -> 0 us
  Pallas kernels: 0 us -> 71.4 us
  matrix products: 17.7 us -> 0 us
  between operations: 13.5 us -> 0.01 us
  local copies, waits for them, and re-layouts: 16 us -> 4.85 us
  other arithmetic: 7.76 us -> 0 us
  blocking collectives: 6.64 us -> 0 us
  starting transfers between devices: 5.96 us -> 0 us
    pallas_call x0 -> x1, Pallas kernels: none -> 71.4 us  [fused(): pl.pallas_call(functools.partial(layer_kernel, count, depth_chunks, row_c...]
    all_to_all x1 -> x0, waiting for transfers between devices: 68.5 us -> none  [shards(): lax.all_to_all(outputs, 'expert', split_axis=0, concat_axis=0, tiled=True)]
    all_gather x2 -> x0, waiting for transfers between devices: 21.1 us -> none  [the longest x1 20.4 us: shards(): inputs = lax.all_gather(slot_rows, 'helper', axis=0, tiled=True)]
    dot_general x3 -> x0, matrix products: 17.7 us -> none  [the longest x1 7.33 us: shards(): jnp.dot(own_rows, lax.all_gather(down_part, 'helper', axis=0, tiled=True)...]
    gather x6 -> x0, local copies, waits for them, and re-layouts: 8.53 us -> none  [the longest x1 6.49 us: shards(): picked = received[local_slot]]
    reduce_sum x2 -> x0, other arithmetic: 7.6 us -> none  [the longest x1 7.59 us: shards(): jnp.sum(gate_values[:, :, None] * picked.astype(jnp.float32), axis=1)]
    all_to_all x1 -> x0, blocking collectives: 6.64 us -> none  [shards(): lax.all_to_all(hidden, 'helper', split_axis=0, concat_axis=1, tiled=True)]
    all_to_all x1 -> x0, starting transfers between devices: 5.92 us -> none  [shards(): lax.all_to_all(outputs, 'expert', split_axis=0, concat_axis=0, tiled=True)]
  transfers between devices with their start and end apart: 3 -> 0, of which waited for: 3 -> 0; matrix products, arithmetic and copies ran while one was open for 10% -> 0% of each run, Pallas kernels for 0% -> 0%
where the time goes in v1:
time: 76.5 us; the launch traced here: 76.3 us
  Pallas kernels  71.4 us (93%)
  local copies, waits for them, and re-layouts  4.85 us (6%)
    pallas_call x1, Pallas kernels, fused(): pl.pallas_call(functools.partial(layer_kernel, count, depth_chunks, row_c...  71.4 us
    unnamed x3, local copies, waits for them, and re-layouts  4.85 us

profile of v1, /device:TPU:0, one launch (start us, length us, event | category | flops | bytes accessed | tf_op | source)
XLA Modules:
  0.0 76.3 jit_solution(10055970565263927198)
XLA Ops:
  0.0 1.4 %copy.7.ex = s32[96,2]{1,0:T(8,128)} copy(s32[96,2]{0,1:T(2,128)} %param.7) | data formatting | bytes 1536 | tf_op args[1]
  1.4 1.4 %copy.8.gv = f32[96,2]{1,0:T(8,128)} copy(f32[96,2]{0,1:T(2,128)} %param.8) | data formatting | bytes 1536 | tf_op args[2]
  2.8 71.4 %expert_layer.1 = bf16[96,4096]{1,0:T(8,128)(2,1)} custom-call(bf16[384,4096]{1,0:T(8,128)(2,1)} %x.1, bf16[4096,384]{1,0:T(8,128)(2,1)} %bitcast.3, bf16[4096,384]{1,0:T(8,128)(2,1)} %bitcast.4, bf16[384,4096]{1,0:T(8,128)(2,1)} %bitcast.5, s32[96,2]{1,0:T(8,128)} %copy.7.ex, f32[96,2]{1,0:T(8,128)} %copy.8.gv), custom_call_target="tpu_custom_call" | custom-call | tf_op jit(solution)/shard_map/expert_layer/pallas_call | solution.py:289
  74.2 2.1 %copy.10 = bf16[96,4096]{1,0:T(8,128)(2,1)} copy(bf16[96,4096]{1,0:T(8,128)(2,1)} %expert_layer.1) | data formatting | bytes 1572864

commit v2 on v1

--- a/solution.py
+++ b/solution.py
@@ -22,24 +22,25 @@
 
 
 def weights_of(experts, gates, expert_count, width, first, slots):
-    rows, top = experts.shape
-    names = lax.broadcasted_iota(jnp.int32, (rows, expert_count), 1)
-    chosen = [(experts[:, k:k + 1] == names).astype(jnp.float32) for k in range(top)]
+    top, rows = experts.shape
+    names = lax.broadcasted_iota(jnp.int32, (expert_count, rows), 0)
+    chosen = [(experts[k:k + 1] == names).astype(jnp.float32) for k in range(top)]
     earlier = (
         lax.broadcasted_iota(jnp.int32, (rows, rows), 0)
-        > lax.broadcasted_iota(jnp.int32, (rows, rows), 1)
+        < lax.broadcasted_iota(jnp.int32, (rows, rows), 1)
     )
     before = jnp.dot(
+        sum(chosen).astype(jnp.bfloat16),
         earlier.astype(jnp.float32).astype(jnp.bfloat16),
-        sum(chosen).astype(jnp.bfloat16),
         preferred_element_type=jnp.float32,
     )
-    number = lax.broadcasted_iota(jnp.int32, (rows, slots), 1) + first
-    total = jnp.zeros((rows, slots), jnp.float32)
+    number = lax.broadcasted_iota(jnp.int32, (slots, rows), 0) + first
+    total = jnp.zeros((slots, rows), jnp.float32)
     for k in range(top):
-        within = jnp.sum(chosen[k] * before, axis=1, keepdims=True).astype(jnp.int32)
-        slot = experts[:, k:k + 1] * width + within
-        total = total + jnp.where(number == slot, gates[:, k:k + 1], 0.0)
+        within = jnp.sum(chosen[k] * before, axis=0, keepdims=True).astype(jnp.int32)
+        slot = experts[k:k + 1] * width + within
+        total = total + jnp.where(number == slot, gates[k:k + 1], 0.0)
+    total = total.T
     high = total.astype(jnp.bfloat16)
     return high, (total - high.astype(jnp.float32)).astype(jnp.bfloat16)
 
@@ -65,15 +66,20 @@
     is_relay = z == inner
     far_first = (1 - side) * lines
     near_slots = half * slots
-    tokens = ex.shape[0]
     depth = width // depth_chunks
-    part_rows = rows // row_chunks
+    part_rows = near_slots
+    far_row, near_row = (1 - side) * near_slots, side * near_slots
+    parts = (pl.multiple_of(far_row, 16), pl.multiple_of(near_row, 16))
     cols_of = width // chunks
 
     def load(k):
         ks = pl.ds(k * depth if isinstance(k, int) else pl.multiple_of(k * depth, depth), depth)
         return (
-            pltpu.make_async_copy(x.at[:, ks], own.at[:, ks], load_sem.at[0, k]),
+            pltpu.make_async_copy(
+                x.at[pl.ds(parts[0], part_rows), ks],
+                own.at[pl.ds(parts[0], part_rows), ks],
+                load_sem.at[0, k],
+            ),
             pltpu.make_async_copy(gw.at[ks], gb.at[ks], load_sem.at[1, k]),
             pltpu.make_async_copy(uw.at[ks], ub.at[ks], load_sem.at[2, k]),
         )
@@ -83,6 +89,9 @@
             copy.start()
     down_load = pltpu.make_async_copy(dw, db, d_sem.at[0])
     down_load.start()
+    rest = pl.ds(parts[1], part_rows)
+    rest_load = pltpu.make_async_copy(x.at[rest], own.at[rest], d_sem.at[3])
+    rest_load.start()
 
     barrier = pltpu.get_barrier_semaphore()
     for step in range(1, count):
@@ -93,11 +102,10 @@
     pl.semaphore_wait(barrier, count)
 
     def rows_copy(r):
-        rs = pl.ds(r * part_rows, part_rows)
+        rs = pl.ds(parts[r], part_rows)
         return remote(x.at[rs], other.at[rs], x_send.at[r], x_recv.at[r], helper=1 - h)
 
-    for r in range(row_chunks):
-        rows_copy(r).start()
+    rows_copy(0).start()
     down_copy = remote(dw, dp, d_sem.at[1], d_sem.at[2], helper=1 - h)
     down_copy.start()
 
@@ -109,42 +117,28 @@
     for copy in notes:
         copy.start()
 
-    def activate(source, first, size, target, waits):
-        acc_g[pl.ds(0, size)] = jnp.zeros((size, acc_g.shape[1]), jnp.float32)
-        acc_u[pl.ds(0, size)] = jnp.zeros((size, acc_u.shape[1]), jnp.float32)
+    def activate(source, first, target, waits):
+        acc_g[...] = jnp.zeros_like(acc_g)
+        acc_u[...] = jnp.zeros_like(acc_u)
 
         def step(k, carry):
             ks = pl.ds(pl.multiple_of(k * depth, depth), depth)
             if waits:
                 for copy in load(k):
                     copy.wait()
-            block = source[pl.ds(first, size), ks]
-            acc_g[pl.ds(0, size)] += jnp.dot(block, gb[ks], preferred_element_type=jnp.float32)
-            acc_u[pl.ds(0, size)] += jnp.dot(block, ub[ks], preferred_element_type=jnp.float32)
+            block = source[pl.ds(first, part_rows), ks]
+            acc_g[...] += jnp.dot(block, gb[ks], preferred_element_type=jnp.float32)
+            acc_u[...] += jnp.dot(block, ub[ks], preferred_element_type=jnp.float32)
             return carry
 
         lax.fori_loop(0, depth_chunks, step, 0)
-        gated = acc_g[pl.ds(0, size)]
-        hidden = gated / (1.0 + jnp.exp(-gated)) * acc_u[pl.ds(0, size)]
-        target[pl.ds(first, size)] = hidden.astype(jnp.bfloat16)
-
-    activate(own, 0, rows, mine, True)
+        gated = acc_g[...]
+        hidden = gated / (1.0 + jnp.exp(-gated)) * acc_u[...]
+        target[pl.ds(first, part_rows)] = hidden.astype(jnp.bfloat16)
 
     def hidden_copy(r):
-        rs = pl.ds(r * part_rows, part_rows)
+        rs = pl.ds(parts[r], part_rows)
         return remote(give.at[rs], theirs.at[rs], h_send.at[r], h_recv.at[r], helper=1 - h)
-
-    for r in range(row_chunks):
-        rows_copy(r).wait_recv()
-        activate(other, r * part_rows, part_rows, give, False)
-        hidden_copy(r).start()
-
-    w_near[0], w_near[1] = weights_of(ex[...], gv[...], count, slots, side * near_slots, near_slots)
-
-    down_load.wait()
-    down_copy.wait_recv()
-    for r in range(row_chunks):
-        hidden_copy(r).wait_recv()
 
     def columns(c):
         return pl.ds(pl.multiple_of(c * cols_of, cols_of), cols_of)
@@ -179,11 +173,24 @@
             p_send.at[c, l], p_recv.at[c], expert=goal,
         )
 
+    def project(r, cs):
+        rs = pl.ds(parts[r], part_rows)
+        value = jnp.dot(mine[rs], db[:, cs], preferred_element_type=jnp.float32)
+        value += jnp.dot(theirs[rs], dp[:, cs], preferred_element_type=jnp.float32)
+        outb[rs, cs] = value.astype(jnp.bfloat16)
+
+    activate(own, parts[0], mine, True)
+    rows_copy(0).wait_recv()
+    activate(other, parts[0], give, False)
+    hidden_copy(0).start()
+    rows_copy(1).start()
+    w_near[0], w_near[1] = weights_of(ex[...], gv[...], count, slots, near_row, near_slots)
+    down_load.wait()
+    down_copy.wait_recv()
+    hidden_copy(0).wait_recv()
+
     def lower(c, carry):
-        cs = columns(c)
-        value = jnp.dot(mine[...], db[:, cs], preferred_element_type=jnp.float32)
-        value += jnp.dot(theirs[...], dp[:, cs], preferred_element_type=jnp.float32)
-        outb[:, cs] = value.astype(jnp.bfloat16)
+        project(0, columns(c))
         for l in range(lines):
             for step in range(COLUMNS):
                 local, away = to_relay(c, l, step)
@@ -201,12 +208,11 @@
 
     lax.fori_loop(0, chunks, lower, 0)
 
-    def send_near(c, carry):
-        for step in range(half):
-            to_near(c, step).start()
-        return carry
-
-    lax.fori_loop(0, chunks, send_near, 0)
+    rest_load.wait()
+    activate(own, parts[1], mine, False)
+    rows_copy(1).wait_recv()
+    activate(other, parts[1], give, False)
+    hidden_copy(1).start()
 
     @pl.when(is_relay)
     def _():
@@ -214,9 +220,21 @@
             arrival(far_ex.at[l], m_recv.at[l, 0]).wait()
             arrival(far_gv.at[l], m_recv.at[l, 1]).wait()
             w_far[l, 0], w_far[l, 1] = weights_of(
-                far_ex[l], far_gv[l], count, slots, side * near_slots, near_slots
+                far_ex[l], far_gv[l], count, slots, near_row, near_slots
             )
 
+    hidden_copy(1).wait_recv()
+
+    def send_near(c, carry):
+        project(1, columns(c))
+        for step in range(half):
+            to_near(c, step).start()
+        return carry
+
+    lax.fori_loop(0, chunks, send_near, 0)
+
+    @pl.when(is_relay)
+    def _():
         def relay(c, carry):
             cs = columns(c)
             for l in range(lines):
@@ -298,8 +316,8 @@
             pltpu.VMEM((width, units), bf16),
             pltpu.VMEM((units, width), bf16),
             pltpu.VMEM((units, width), bf16),
-            pltpu.VMEM((rows, units), f32),
-            pltpu.VMEM((rows, units), f32),
+            pltpu.VMEM((near_slots, units), f32),
+            pltpu.VMEM((near_slots, units), f32),
             pltpu.VMEM((rows, units), bf16),
             pltpu.VMEM((rows, units), bf16),
             pltpu.VMEM((rows, units), bf16),
@@ -308,14 +326,14 @@
             pltpu.VMEM((lines, tokens, width), bf16),
             pltpu.VMEM((near_slots, width), bf16),
             pltpu.VMEM((tokens, width), bf16),
-            pltpu.VMEM((lines, tokens, top), jnp.int32),
-            pltpu.VMEM((lines, tokens, top), f32),
+            pltpu.VMEM((lines, top, tokens), jnp.int32),
+            pltpu.VMEM((lines, top, tokens), f32),
             pltpu.VMEM((2, tokens, near_slots), bf16),
             pltpu.VMEM((lines, 2, tokens, near_slots), bf16),
             dma((3, depth_chunks)),
             dma((row_chunks,)), dma((row_chunks,)),
             dma((row_chunks,)), dma((row_chunks,)),
-            dma((3,)),
+            dma((4,)),
             dma((2,)), dma((lines, 2)),
             dma((chunks, lines, COLUMNS)), dma((chunks, lines, half)),
             dma((chunks, half)), dma((chunks, half)),
@@ -330,8 +348,8 @@
         gate_weight.reshape(gate_weight.shape[1:]),
         up_weight.reshape(up_weight.shape[1:]),
         down_weight.reshape(down_weight.shape[1:]),
-        experts,
-        gate_values,
+        experts.T,
+        gate_values.T,
     )
 
 

time: 76.5 us -> 70.9 us (0.927)
  local copies, waits for them, and re-layouts: 4.85 us -> 2.06 us
  Pallas kernels: 71.4 us -> 68.7 us
    unnamed x3 -> x1, local copies, waits for them, and re-layouts: 4.85 us -> 2.06 us
    pallas_call x1, Pallas kernels: 71.4 us -> 68.7 us  [fused(): pl.pallas_call(functools.partial(layer_kernel, count, depth_chunks, row_c...]
where the time goes in v2:
time: 70.9 us; the launch traced here: 70.7 us
  Pallas kernels  68.7 us (97%)
  local copies, waits for them, and re-layouts  2.06 us (3%)
    pallas_call x1, Pallas kernels, fused(): pl.pallas_call(functools.partial(layer_kernel, count, depth_chunks, row_c...  68.7 us
    unnamed x1, local copies, waits for them, and re-layouts  2.06 us

profile of v2, /device:TPU:0, one launch (start us, length us, event | category | flops | bytes accessed | tf_op | source)
XLA Modules:
  0.0 70.7 jit_solution(12155968132826576662)
XLA Ops:
  0.0 68.7 %expert_layer.1 = bf16[96,4096]{1,0:T(8,128)(2,1)} custom-call(bf16[384,4096]{1,0:T(8,128)(2,1)} %x.1, bf16[4096,384]{1,0:T(8,128)(2,1)} %bitcast.5, bf16[4096,384]{1,0:T(8,128)(2,1)} %bitcast.6, bf16[384,4096]{1,0:T(8,128)(2,1)} %bitcast.7, s32[2,96]{1,0:T(2,128)} %bitcast.8, f32[2,96]{1,0:T(2,128)} %bitcast.9), custom_call_target="tpu_custom_call" | custom-call | tf_op jit(solution)/shard_map/expert_layer/pallas_call | solution.py:307
  68.7 2.1 %copy.8 = bf16[96,4096]{1,0:T(8,128)(2,1)} copy(bf16[96,4096]{1,0:T(8,128)(2,1)} %expert_layer.1) | data formatting | bytes 1572864

commit v3 on v2

--- a/solution.py
+++ b/solution.py
@@ -50,7 +50,7 @@
     x, gw, uw, dw, ex, gv, out,
     own, other, gb, ub, db, dp, acc_g, acc_u, give, mine, theirs,
     outb, relayed, partial, near, far, far_ex, far_gv, w_near, w_far,
-    load_sem, x_send, x_recv, h_send, h_recv, d_sem,
+    load_sem, x_load, x_send, x_recv, h_send, h_recv, d_sem,
     m_send, m_recv, f_send, f_recv, n_send, n_recv, p_send, p_recv,
 ):
     e, h = lax.axis_index("expert"), lax.axis_index("helper")
@@ -87,11 +87,27 @@
     for k in range(depth_chunks):
         for copy in load(k):
             copy.start()
-    down_load = pltpu.make_async_copy(dw, db, d_sem.at[0])
-    down_load.start()
     rest = pl.ds(parts[1], part_rows)
-    rest_load = pltpu.make_async_copy(x.at[rest], own.at[rest], d_sem.at[3])
-    rest_load.start()
+    rest_load = pltpu.make_async_copy(x.at[rest], own.at[rest], x_load.at[0])
+
+    def columns(c):
+        return pl.ds(pl.multiple_of(c * cols_of, cols_of), cols_of)
+
+    def down_load(c):
+        return pltpu.make_async_copy(dw.at[:, columns(c)], db.at[:, columns(c)], d_sem.at[0, c])
+
+    def down_copy(c):
+        return remote(
+            dw.at[:, columns(c)], dp.at[:, columns(c)], d_sem.at[1, c], d_sem.at[2, c],
+            helper=1 - h,
+        )
+
+    def each(first, last, action):
+        def step(c, carry):
+            action(c)
+            return carry
+
+        lax.fori_loop(first, last, step, 0)
 
     barrier = pltpu.get_barrier_semaphore()
     for step in range(1, count):
@@ -106,8 +122,8 @@
         return remote(x.at[rs], other.at[rs], x_send.at[r], x_recv.at[r], helper=1 - h)
 
     rows_copy(0).start()
-    down_copy = remote(dw, dp, d_sem.at[1], d_sem.at[2], helper=1 - h)
-    down_copy.start()
+    early = chunks // 2
+    each(0, early, lambda c: down_copy(c).start())
 
     far_relay = (lines - side) * COLUMNS + y
     notes = (
@@ -140,9 +156,6 @@
         rs = pl.ds(parts[r], part_rows)
         return remote(give.at[rs], theirs.at[rs], h_send.at[r], h_recv.at[r], helper=1 - h)
 
-    def columns(c):
-        return pl.ds(pl.multiple_of(c * cols_of, cols_of), cols_of)
-
     def rows_at(index):
         return pl.ds(pl.multiple_of(index * slots, slots), slots)
 
@@ -180,16 +193,19 @@
         outb[rs, cs] = value.astype(jnp.bfloat16)
 
     activate(own, parts[0], mine, True)
+    each(0, chunks, lambda c: down_load(c).start())
+    rest_load.start()
     rows_copy(0).wait_recv()
     activate(other, parts[0], give, False)
     hidden_copy(0).start()
+    each(early, chunks, lambda c: down_copy(c).start())
     rows_copy(1).start()
     w_near[0], w_near[1] = weights_of(ex[...], gv[...], count, slots, near_row, near_slots)
-    down_load.wait()
-    down_copy.wait_recv()
     hidden_copy(0).wait_recv()
 
     def lower(c, carry):
+        down_load(c).wait()
+        down_copy(c).wait_recv()
         project(0, columns(c))
         for l in range(lines):
             for step in range(COLUMNS):
@@ -285,7 +301,7 @@
     for r in range(row_chunks):
         rows_copy(r).wait_send()
         hidden_copy(r).wait_send()
-    down_copy.wait_send()
+    each(0, chunks, lambda c: down_copy(c).wait_send())
     for copy in notes:
         copy.wait_send()
 
@@ -299,7 +315,7 @@
     half = count // 2
     lines = half // COLUMNS
     near_slots = half * slots
-    depth_chunks, row_chunks, chunks = 4, 2, 8
+    depth_chunks, row_chunks, chunks = 4, 2, 4
     bf16, f32 = jnp.bfloat16, jnp.float32
     dma = pltpu.SemaphoreType.DMA
     vmem = pl.BlockSpec(memory_space=pltpu.VMEM)
@@ -330,17 +346,17 @@
             pltpu.VMEM((lines, top, tokens), f32),
             pltpu.VMEM((2, tokens, near_slots), bf16),
             pltpu.VMEM((lines, 2, tokens, near_slots), bf16),
-            dma((3, depth_chunks)),
+            dma((3, depth_chunks)), dma((1,)),
             dma((row_chunks,)), dma((row_chunks,)),
             dma((row_chunks,)), dma((row_chunks,)),
-            dma((4,)),
+            dma((3, chunks)),
             dma((2,)), dma((lines, 2)),
             dma((chunks, lines, COLUMNS)), dma((chunks, lines, half)),
             dma((chunks, half)), dma((chunks, half)),
             dma((chunks, lines)), dma((chunks,)),
         ],
         compiler_params=pltpu.CompilerParams(
-            collective_id=0, has_side_effects=True, vmem_limit_bytes=60 << 20
+            collective_id=0, has_side_effects=True, vmem_limit_bytes=53 << 20
         ),
         name="expert_layer",
     )(

time: 70.9 us -> 67.6 us (0.953)
  Pallas kernels: 68.7 us -> 65.2 us
    pallas_call x1, Pallas kernels: 68.7 us -> 65.2 us  [fused(): pl.pallas_call(functools.partial(layer_kernel, count, depth_chunks, row_c...]
    unnamed x1 -> x5, local copies, waits for them, and re-layouts: 2.06 us -> 2.24 us
where the time goes in v3:
time: 67.6 us; the launch traced here: 67.5 us
  Pallas kernels  65.2 us (96%)
  local copies, waits for them, and re-layouts  2.24 us (3%)
    pallas_call x1, Pallas kernels, fused(): pl.pallas_call(functools.partial(layer_kernel, count, depth_chunks, row_c...  65.2 us
    unnamed x5, local copies, waits for them, and re-layouts  2.24 us

profile of v3, /device:TPU:0, one launch (start us, length us, event | category | flops | bytes accessed | tf_op | source)
XLA Modules:
  0.0 67.5 jit_solution(15100229097969514088)
XLA Ops:
  0.0 0.0 copy-start
  0.0 0.7 %copy-done = s32[96,2]{0,1:T(2,128)S(1)} copy-done((s32[96,2]{0,1:T(2,128)S(1)}, s32[96,2]{0,1:T(2,128)}, u32[]{:S(2)}) %copy-start) | copy-done | bytes 792
  0.7 0.0 copy-start.1
  0.7 0.7 %copy-done.1 = f32[96,2]{0,1:T(2,128)S(1)} copy-done((f32[96,2]{0,1:T(2,128)S(1)}, f32[96,2]{0,1:T(2,128)}, u32[]{:S(2)}) %copy-start.1) | copy-done | bytes 792
  1.4 65.2 %expert_layer.1 = bf16[96,4096]{1,0:T(8,128)(2,1)S(1)} custom-call(bf16[384,4096]{1,0:T(8,128)(2,1)} %x.1, bf16[4096,384]{1,0:T(8,128)(2,1)} %bitcast.7, bf16[4096,384]{1,0:T(8,128)(2,1)} %bitcast.8, bf16[384,4096]{1,0:T(8,128)(2,1)} %bitcast.9, s32[2,96]{1,0:T(2,128)S(1)} %bitcast.5, f32[2,96]{1,0:T(2,128)S(1)} %bitcast.6), custom_call_target="tpu_custom_call" | custom-call | tf_op jit(solution)/shard_map/expert_layer/pallas_call | solution.py:323
  66.6 0.9 %copy.8 = bf16[96,4096]{1,0:T(8,128)(2,1)} copy(bf16[96,4096]{1,0:T(8,128)(2,1)S(1)} %expert_layer.1) | data formatting | bytes 1572864
Async XLA Ops:
  0.0 0.7 %copy-start = (s32[96,2]{0,1:T(2,128)S(1)}, s32[96,2]{0,1:T(2,128)}, u32[]{:S(2)}) copy-start(s32[96,2]{0,1:T(2,128)} %param.7) | copy-start | bytes 2308
  0.7 0.7 %copy-start.1 = (f32[96,2]{0,1:T(2,128)S(1)}, f32[96,2]{0,1:T(2,128)}, u32[]{:S(2)}) copy-start(f32[96,2]{0,1:T(2,128)} %param.8) | copy-start | bytes 2308
